TPU v7x, 128 devices: a whole 4x4x4 slice. The times are simulated.
128 devices in a mesh: grp: 8 (over z_lo, x), obs: 16 (over y, z_hi, core).
Axes of the slice: x: 4, y: 4, z: 4 (z_hi: 2, z_lo: 2; z = z_hi * 2 + z_lo), core: 2. Of those that a mesh axis runs over, the one named last changes fastest.
Arguments:
- signals: bfloat16 [4, 256, 131072], P(None, None, ('grp', 'obs')), may hold values from -6 to 6
- patch_count: int32 [128], P(('grp', 'obs')), may hold values from 0 to 8, as said below
- patch_place: int32 [1024], P(('grp', 'obs')), may hold values from 0 to 63, as said below
- face_geom: float32 [4, 65536], P(None, ('grp', 'obs')), may hold values from -3.5 to 30, as said below
- obs_pos: float32 [3, 4096], P(None, 'obs'), may hold values from -60 to 60, as said below
Outputs:
- pressure: float32 [16, 4096], P('grp', 'obs')
Inputs may be any that keep to these rules, and one draw needn't show every extreme that they name: `patch_count`: each partition holds 0 to 8 live patches; in every face group the counts sum to 64 and some partition holds exactly 8. `patch_place`: A live slot names owner o and patch j of the partition's group as o * 4 + j; within a group every such value is named by exactly one live slot, so every owner receives exactly 4 patches; no partition holds two live patches of the same owner. Slots beyond the count hold arbitrary values in the range. `face_geom`: faces lie on a surface around the first coordinate's axis: the first coordinate between 0 and 30, the distance from that axis between 2 and 3.5; the area lies between 0.5 and 10. `obs_pos`: every observer lies 25 to 60 from the anchor (0, 0, 0) and 8 or more from the first coordinate's axis.
All inputs are finite; a program needn't handle non-finite values.
Results may differ from a plain program's by a relative error of at most 0.004.
Values may be sent and summed in bfloat16 or wider, within the bound.
No kernel may reach another device: no remote copies, remote signals or barrier semaphores. Data moves between devices by JAX's collectives and lax.ppermute only.
A program may use at most 64 MiB of HBM per device.

v0:
```python
import math
import jax
import jax.numpy as jnp
from jax import lax
from jax.sharding import PartitionSpec as P

SAMPLES = 256
NFREQ = 8
NSIG = 4
PATCH = 128
MAXP = 8
PER_OWN = 4
FACES_OWN = 512
omega_step = 0.5
four_pi = 4.0 * math.pi


def spectral_basis(samples, freq_count):
    sample_idx = jnp.arange(samples, dtype=jnp.float32)
    harmonic = jnp.arange(1, freq_count + 1, dtype=jnp.float32)
    angles = 2.0 * math.pi / samples * (sample_idx[:, None] * harmonic[None, :])
    window = (0.5 - 0.5 * jnp.cos(2.0 * math.pi / samples * sample_idx)) * math.sqrt(
        8.0 / (3.0 * samples)
    )
    table = jnp.concatenate(
        [window[:, None] * jnp.cos(angles), -window[:, None] * jnp.sin(angles)], axis=1
    )
    return table.astype(jnp.bfloat16)


def pressure_tiles(observers, spectra, geometry):
    freq_count = spectra.shape[0] // 8
    wavenumber = omega_step * jnp.arange(1, freq_count + 1, dtype=jnp.float32)
    values = spectra.reshape(4, 2, freq_count, spectra.shape[1])
    separation = observers[:, :, None] - geometry[:3, None, :]
    dist_sq = jnp.sum(separation * separation, axis=0)
    distance = jnp.sqrt(dist_sq)
    inv_sq = 1.0 / dist_sq
    load_re = jnp.zeros((freq_count,) + dist_sq.shape, jnp.float32)
    load_im = jnp.zeros((freq_count,) + dist_sq.shape, jnp.float32)
    for coord in range(3):
        load_re = load_re + values[1 + coord, 0][:, None, :] * separation[coord][None]
        load_im = load_im + values[1 + coord, 1][:, None, :] * separation[coord][None]
    dip_re = load_re * inv_sq[None]
    dip_im = load_im * inv_sq[None]
    omega_grid = wavenumber[:, None, None]
    phase = omega_grid * distance[None]
    mono_re = values[0, 0][:, None, :]
    mono_im = values[0, 1][:, None, :]
    bracket_re = -omega_grid * mono_im + dip_re - phase * dip_im
    bracket_im = omega_grid * mono_re + dip_im + phase * dip_re
    amplitude = (geometry[3][None, :] / (four_pi * distance))[None]
    green_re = amplitude * jnp.cos(phase)
    green_im = -amplitude * jnp.sin(phase)
    press_re = jnp.sum(green_re * bracket_re - green_im * bracket_im, axis=2)
    press_im = jnp.sum(green_re * bracket_im + green_im * bracket_re, axis=2)
    return jnp.concatenate([press_re, press_im], axis=0)


def accumulate(observers, spectra, geometry):
    face_count = spectra.shape[1]
    block_len = face_count
    while block_len > 128 and (
        block_len * observers.shape[1] > 131072 or face_count % block_len != 0
    ):
        block_len = block_len // 2
    step_count = face_count // block_len
    spec_blocks = spectra.reshape(spectra.shape[0], step_count, block_len).transpose(1, 0, 2)
    geom_blocks = geometry.reshape(4, step_count, block_len).transpose(1, 0, 2)

    def add_block(running, pieces):
        return (running + pressure_tiles(observers, pieces[0], pieces[1]), None)

    zero_sum = jnp.zeros((spectra.shape[0] // 4, observers.shape[1]), jnp.float32)
    result, _ = lax.scan(add_block, zero_sum, (spec_blocks, geom_blocks))
    return result


def local(signals, patch_count, patch_place, face_geom, obs_pos):
    owners = lax.axis_size("obs")
    channels = NSIG * 2 * NFREQ
    dft_basis = spectral_basis(SAMPLES, NFREQ).astype(jnp.float32)
    slot_index = jnp.arange(MAXP, dtype=jnp.int32)
    is_live = slot_index < patch_count[0]
    target_owner = patch_place // PER_OWN
    target_part = patch_place % PER_OWN
    owner_index = jnp.arange(owners, dtype=jnp.int32)
    picked = jnp.logical_and(target_owner[None, :] == owner_index[:, None], is_live[None, :])
    header = jnp.where(
        jnp.any(picked, axis=1), jnp.sum(jnp.where(picked, target_part[None, :], 0), axis=1), -1
    )
    select = picked.astype(jnp.bfloat16)
    row_blocks = signals.reshape(NSIG, SAMPLES, MAXP, PATCH)
    outgoing = jnp.einsum(
        "om,stmp->ostp", select, row_blocks, preferred_element_type=jnp.float32
    ).astype(jnp.bfloat16)
    arrived_rows, senders = (
        lax.all_to_all(outgoing, "obs", split_axis=0, concat_axis=0, tiled=True),
        lax.all_to_all(header, "obs", split_axis=0, concat_axis=0, tiled=True),
    )
    arrived = jnp.einsum(
        "ostp,tc->oscp",
        arrived_rows.astype(jnp.float32),
        dft_basis,
        precision=lax.Precision.HIGHEST,
    ).astype(jnp.bfloat16)
    arrived = arrived.reshape(owners, channels, PATCH)
    owned_part = (senders[:, None] == jnp.arange(PER_OWN, dtype=jnp.int32)[None, :]).astype(
        jnp.bfloat16
    )
    face_spec = jnp.einsum(
        "oj,okp->kjp", owned_part, arrived, preferred_element_type=jnp.float32
    ).astype(jnp.bfloat16)
    face_spec = face_spec.reshape(channels, FACES_OWN)
    spec_wide = face_spec.astype(jnp.float32)
    pressure = accumulate(
        obs_pos,
        lax.all_gather(spec_wide, "obs", axis=1, tiled=True),
        lax.all_gather(face_geom, "obs", axis=1, tiled=True),
    )
    rows_out = 2 * NFREQ // lax.axis_size("grp")
    summed = lax.psum(pressure, "grp")
    return lax.dynamic_slice_in_dim(summed, lax.axis_index("grp") * rows_out, rows_out, 0)


def solution(mesh):
    return jax.shard_map(
        local,
        mesh=mesh,
        in_specs=(
            P(None, None, ("grp", "obs")),
            P(("grp", "obs")),
            P(("grp", "obs")),
            P(None, ("grp", "obs")),
            P(None, "obs"),
        ),
        out_specs=P("grp", "obs"),
        check_vma=False,
    )
```

profile of v0, /device:TPU:0, one launch (start us, length us, event | category | flops | bytes accessed | tf_op | source)
XLA Modules:
  0.0 536.7 jit_solution(8264392097134709399)
XLA Ops:
  8.7 8.0 %all-to-all-start.1 = ((s32[16,1,1]{2,1,0:T(1,128)}), s32[16,1,1]{2,1,0:T(1,128)S(1)}, u32[]{:S(2)}, u32[]{:S(2)}) async-start(s32[16,1,1]{2,1,0:T(1,128)} %copy.22), calls=%async_computation.1 | async-start | bytes 16384 | tf_op jit(solution)/shard_map/all_to_all | solution.py:99
  24.3 6.3 %all-to-all-start = ((bf16[16,4,256,128]{3,2,1,0:T(8,128)(2,1)}), bf16[16,4,256,128]{3,2,1,0:T(8,128)(2,1)}, u32[]{:S(2)}, u32[]{:S(2)}) async-start(bf16[16,4,256,128]{3,2,1,0:T(8,128)(2,1)} %copy.21), calls=%async_computation | async-start | bytes 8388608 | tf_op jit(solution)/shard_map/all_to_all | solution.py:98
  31.2 52.9 %all-to-all-done = bf16[16,4,256,128]{3,2,1,0:T(8,128)(2,1)} async-done(((bf16[16,4,256,128]{3,2,1,0:T(8,128)(2,1)}), bf16[16,4,256,128]{3,2,1,0:T(8,128)(2,1)}, u32[]{:S(2)}, u32[]{:S(2)}) %all-to-all-start) | async-done | bytes 4194336 | tf_op jit(solution)/shard_map/all_to_all | solution.py:98
  88.0 28.8 %all_gather.6 = f32[4,8192]{1,0:T(4,128)S(1)} all-gather(f32[4,512]{1,0:T(4,128)S(1)} %copy-done.1), channel_id=1, replica_groups=mesh['grp'=8,'obs'=16] {'obs'}, dimensions={1}, use_global_device_ids=true | all-gather | bytes 139264 | tf_op jit(solution)/shard_map/all_gather | solution.py:119
  116.8 27.1 %all-gather.2.cloned.1.call-done = f32[64,8192]{1,0:T(8,128)} async-done(((f32[64,512]{1,0:T(8,128)}), f32[64,8192]{1,0:T(8,128)}) %all-gather.2.cloned.1.call-update) | async-done | bytes 2097168 | tf_op jit(solution)/shard_map/all_gather | solution.py:118
  143.9 4.1 copy.30
  148.0 348.0 %while.11 = (s32[]{:T(128)}, f32[16,256]{1,0:T(8,128)S(1)}, f32[16,4,512]{2,1,0:T(4,128)S(1)}, f32[3,256]{1,0:T(4,128)S(1)}, f32[16,64,512]{2,0,1:T(8,128)}, /*index=5*/s32[]{:T(128)}, s32[]{:T(128)}, s32[]{}) while((s32[]{:T(128)}, f32[16,256]{1,0:T(8,128)S(1)}, f32[16,4,512]{2,1,0:T(4,128)S(1)}, f32[3,256]{1,0:T(4,128)S(1)}, ...), condition=%wide.region_6.7_spmd.clone, body=%wide.region_2.6_spmd.clone.sunk | while | flops 31997980 | bytes 12545307 | solution.py:75
  150.2 19.5 %fusion.38 = (f32[8,256]{1,0:T(8,128)S(1)}, f32[8,256]{1,0:T(8,128)S(1)}) fusion(f32[8,512]{1,0:T(8,128)S(1)} %get-tuple-element.167, f32[256,512]{1,0:T(8,128)S(1)} %get-tuple-element.169, f32[8,512]{1,0:T(8,128)S(1)} %get-tuple-element.170, f32[8,512]{1,0:T(8,128)S(1)} %get-tuple-element.171, f32[8,512]{1,0:T(8,128)S(1)} %get-tuple-element.172, ...), kind=kLoop, calls=%fused_computation.8.clone.1 | loop fusion | flops 30404608 | bytes 3817504 | tf_op jit(solution)/shard_map/while/body/eval_jaxpr/reduce_sum | solution.py:55
  172.0 19.5 %fusion.38 = (f32[8,256]{1,0:T(8,128)S(1)}, f32[8,256]{1,0:T(8,128)S(1)}) fusion(f32[8,512]{1,0:T(8,128)S(1)} %get-tuple-element.167, f32[256,512]{1,0:T(8,128)S(1)} %get-tuple-element.169, f32[8,512]{1,0:T(8,128)S(1)} %get-tuple-element.170, f32[8,512]{1,0:T(8,128)S(1)} %get-tuple-element.171, f32[8,512]{1,0:T(8,128)S(1)} %get-tuple-element.172, ...), kind=kLoop, calls=%fused_computation.8.clone.1 | loop fusion | flops 30404608 | bytes 3817504 | tf_op jit(solution)/shard_map/while/body/eval_jaxpr/reduce_sum | solution.py:55
  193.7 19.5 %fusion.38 = (f32[8,256]{1,0:T(8,128)S(1)}, f32[8,256]{1,0:T(8,128)S(1)}) fusion(f32[8,512]{1,0:T(8,128)S(1)} %get-tuple-element.167, f32[256,512]{1,0:T(8,128)S(1)} %get-tuple-element.169, f32[8,512]{1,0:T(8,128)S(1)} %get-tuple-element.170, f32[8,512]{1,0:T(8,128)S(1)} %get-tuple-element.171, f32[8,512]{1,0:T(8,128)S(1)} %get-tuple-element.172, ...), kind=kLoop, calls=%fused_computation.8.clone.1 | loop fusion | flops 30404608 | bytes 3817504 | tf_op jit(solution)/shard_map/while/body/eval_jaxpr/reduce_sum | solution.py:55
  215.5 19.5 %fusion.38 = (f32[8,256]{1,0:T(8,128)S(1)}, f32[8,256]{1,0:T(8,128)S(1)}) fusion(f32[8,512]{1,0:T(8,128)S(1)} %get-tuple-element.167, f32[256,512]{1,0:T(8,128)S(1)} %get-tuple-element.169, f32[8,512]{1,0:T(8,128)S(1)} %get-tuple-element.170, f32[8,512]{1,0:T(8,128)S(1)} %get-tuple-element.171, f32[8,512]{1,0:T(8,128)S(1)} %get-tuple-element.172, ...), kind=kLoop, calls=%fused_computation.8.clone.1 | loop fusion | flops 30404608 | bytes 3817504 | tf_op jit(solution)/shard_map/while/body/eval_jaxpr/reduce_sum | solution.py:55
  237.2 19.5 %fusion.38 = (f32[8,256]{1,0:T(8,128)S(1)}, f32[8,256]{1,0:T(8,128)S(1)}) fusion(f32[8,512]{1,0:T(8,128)S(1)} %get-tuple-element.167, f32[256,512]{1,0:T(8,128)S(1)} %get-tuple-element.169, f32[8,512]{1,0:T(8,128)S(1)} %get-tuple-element.170, f32[8,512]{1,0:T(8,128)S(1)} %get-tuple-element.171, f32[8,512]{1,0:T(8,128)S(1)} %get-tuple-element.172, ...), kind=kLoop, calls=%fused_computation.8.clone.1 | loop fusion | flops 30404608 | bytes 3817504 | tf_op jit(solution)/shard_map/while/body/eval_jaxpr/reduce_sum | solution.py:55
  259.0 19.5 %fusion.38 = (f32[8,256]{1,0:T(8,128)S(1)}, f32[8,256]{1,0:T(8,128)S(1)}) fusion(f32[8,512]{1,0:T(8,128)S(1)} %get-tuple-element.167, f32[256,512]{1,0:T(8,128)S(1)} %get-tuple-element.169, f32[8,512]{1,0:T(8,128)S(1)} %get-tuple-element.170, f32[8,512]{1,0:T(8,128)S(1)} %get-tuple-element.171, f32[8,512]{1,0:T(8,128)S(1)} %get-tuple-element.172, ...), kind=kLoop, calls=%fused_computation.8.clone.1 | loop fusion | flops 30404608 | bytes 3817504 | tf_op jit(solution)/shard_map/while/body/eval_jaxpr/reduce_sum | solution.py:55
  280.7 19.5 %fusion.38 = (f32[8,256]{1,0:T(8,128)S(1)}, f32[8,256]{1,0:T(8,128)S(1)}) fusion(f32[8,512]{1,0:T(8,128)S(1)} %get-tuple-element.167, f32[256,512]{1,0:T(8,128)S(1)} %get-tuple-element.169, f32[8,512]{1,0:T(8,128)S(1)} %get-tuple-element.170, f32[8,512]{1,0:T(8,128)S(1)} %get-tuple-element.171, f32[8,512]{1,0:T(8,128)S(1)} %get-tuple-element.172, ...), kind=kLoop, calls=%fused_computation.8.clone.1 | loop fusion | flops 30404608 | bytes 3817504 | tf_op jit(solution)/shard_map/while/body/eval_jaxpr/reduce_sum | solution.py:55
  302.5 19.5 %fusion.38 = (f32[8,256]{1,0:T(8,128)S(1)}, f32[8,256]{1,0:T(8,128)S(1)}) fusion(f32[8,512]{1,0:T(8,128)S(1)} %get-tuple-element.167, f32[256,512]{1,0:T(8,128)S(1)} %get-tuple-element.169, f32[8,512]{1,0:T(8,128)S(1)} %get-tuple-element.170, f32[8,512]{1,0:T(8,128)S(1)} %get-tuple-element.171, f32[8,512]{1,0:T(8,128)S(1)} %get-tuple-element.172, ...), kind=kLoop, calls=%fused_computation.8.clone.1 | loop fusion | flops 30404608 | bytes 3817504 | tf_op jit(solution)/shard_map/while/body/eval_jaxpr/reduce_sum | solution.py:55
  324.2 19.5 %fusion.38 = (f32[8,256]{1,0:T(8,128)S(1)}, f32[8,256]{1,0:T(8,128)S(1)}) fusion(f32[8,512]{1,0:T(8,128)S(1)} %get-tuple-element.167, f32[256,512]{1,0:T(8,128)S(1)} %get-tuple-element.169, f32[8,512]{1,0:T(8,128)S(1)} %get-tuple-element.170, f32[8,512]{1,0:T(8,128)S(1)} %get-tuple-element.171, f32[8,512]{1,0:T(8,128)S(1)} %get-tuple-element.172, ...), kind=kLoop, calls=%fused_computation.8.clone.1 | loop fusion | flops 30404608 | bytes 3817504 | tf_op jit(solution)/shard_map/while/body/eval_jaxpr/reduce_sum | solution.py:55
  346.0 19.5 %fusion.38 = (f32[8,256]{1,0:T(8,128)S(1)}, f32[8,256]{1,0:T(8,128)S(1)}) fusion(f32[8,512]{1,0:T(8,128)S(1)} %get-tuple-element.167, f32[256,512]{1,0:T(8,128)S(1)} %get-tuple-element.169, f32[8,512]{1,0:T(8,128)S(1)} %get-tuple-element.170, f32[8,512]{1,0:T(8,128)S(1)} %get-tuple-element.171, f32[8,512]{1,0:T(8,128)S(1)} %get-tuple-element.172, ...), kind=kLoop, calls=%fused_computation.8.clone.1 | loop fusion | flops 30404608 | bytes 3817504 | tf_op jit(solution)/shard_map/while/body/eval_jaxpr/reduce_sum | solution.py:55
  367.7 19.5 %fusion.38 = (f32[8,256]{1,0:T(8,128)S(1)}, f32[8,256]{1,0:T(8,128)S(1)}) fusion(f32[8,512]{1,0:T(8,128)S(1)} %get-tuple-element.167, f32[256,512]{1,0:T(8,128)S(1)} %get-tuple-element.169, f32[8,512]{1,0:T(8,128)S(1)} %get-tuple-element.170, f32[8,512]{1,0:T(8,128)S(1)} %get-tuple-element.171, f32[8,512]{1,0:T(8,128)S(1)} %get-tuple-element.172, ...), kind=kLoop, calls=%fused_computation.8.clone.1 | loop fusion | flops 30404608 | bytes 3817504 | tf_op jit(solution)/shard_map/while/body/eval_jaxpr/reduce_sum | solution.py:55
  389.5 19.5 %fusion.38 = (f32[8,256]{1,0:T(8,128)S(1)}, f32[8,256]{1,0:T(8,128)S(1)}) fusion(f32[8,512]{1,0:T(8,128)S(1)} %get-tuple-element.167, f32[256,512]{1,0:T(8,128)S(1)} %get-tuple-element.169, f32[8,512]{1,0:T(8,128)S(1)} %get-tuple-element.170, f32[8,512]{1,0:T(8,128)S(1)} %get-tuple-element.171, f32[8,512]{1,0:T(8,128)S(1)} %get-tuple-element.172, ...), kind=kLoop, calls=%fused_computation.8.clone.1 | loop fusion | flops 30404608 | bytes 3817504 | tf_op jit(solution)/shard_map/while/body/eval_jaxpr/reduce_sum | solution.py:55
  411.2 19.5 %fusion.38 = (f32[8,256]{1,0:T(8,128)S(1)}, f32[8,256]{1,0:T(8,128)S(1)}) fusion(f32[8,512]{1,0:T(8,128)S(1)} %get-tuple-element.167, f32[256,512]{1,0:T(8,128)S(1)} %get-tuple-element.169, f32[8,512]{1,0:T(8,128)S(1)} %get-tuple-element.170, f32[8,512]{1,0:T(8,128)S(1)} %get-tuple-element.171, f32[8,512]{1,0:T(8,128)S(1)} %get-tuple-element.172, ...), kind=kLoop, calls=%fused_computation.8.clone.1 | loop fusion | flops 30404608 | bytes 3817504 | tf_op jit(solution)/shard_map/while/body/eval_jaxpr/reduce_sum | solution.py:55
  432.9 19.5 %fusion.38 = (f32[8,256]{1,0:T(8,128)S(1)}, f32[8,256]{1,0:T(8,128)S(1)}) fusion(f32[8,512]{1,0:T(8,128)S(1)} %get-tuple-element.167, f32[256,512]{1,0:T(8,128)S(1)} %get-tuple-element.169, f32[8,512]{1,0:T(8,128)S(1)} %get-tuple-element.170, f32[8,512]{1,0:T(8,128)S(1)} %get-tuple-element.171, f32[8,512]{1,0:T(8,128)S(1)} %get-tuple-element.172, ...), kind=kLoop, calls=%fused_computation.8.clone.1 | loop fusion | flops 30404608 | bytes 3817504 | tf_op jit(solution)/shard_map/while/body/eval_jaxpr/reduce_sum | solution.py:55
  454.7 19.5 %fusion.38 = (f32[8,256]{1,0:T(8,128)S(1)}, f32[8,256]{1,0:T(8,128)S(1)}) fusion(f32[8,512]{1,0:T(8,128)S(1)} %get-tuple-element.167, f32[256,512]{1,0:T(8,128)S(1)} %get-tuple-element.169, f32[8,512]{1,0:T(8,128)S(1)} %get-tuple-element.170, f32[8,512]{1,0:T(8,128)S(1)} %get-tuple-element.171, f32[8,512]{1,0:T(8,128)S(1)} %get-tuple-element.172, ...), kind=kLoop, calls=%fused_computation.8.clone.1 | loop fusion | flops 30404608 | bytes 3817504 | tf_op jit(solution)/shard_map/while/body/eval_jaxpr/reduce_sum | solution.py:55
  476.4 19.5 %fusion.38 = (f32[8,256]{1,0:T(8,128)S(1)}, f32[8,256]{1,0:T(8,128)S(1)}) fusion(f32[8,512]{1,0:T(8,128)S(1)} %get-tuple-element.167, f32[256,512]{1,0:T(8,128)S(1)} %get-tuple-element.169, f32[8,512]{1,0:T(8,128)S(1)} %get-tuple-element.170, f32[8,512]{1,0:T(8,128)S(1)} %get-tuple-element.171, f32[8,512]{1,0:T(8,128)S(1)} %get-tuple-element.172, ...), kind=kLoop, calls=%fused_computation.8.clone.1 | loop fusion | flops 30404608 | bytes 3817504 | tf_op jit(solution)/shard_map/while/body/eval_jaxpr/reduce_sum | solution.py:55
  496.0 33.3 %psum.7 = f32[16,256]{1,0:T(8,128)S(1)} all-reduce(f32[16,256]{1,0:T(8,128)S(1)} %get-tuple-element.32), channel_id=1, replica_groups=mesh['grp'=8,'obs'=16] {'grp'}, use_global_device_ids=true, to_apply=%region_7.8 | all-reduce | flops 4096 | bytes 32768 | tf_op jit(solution)/shard_map/psum | solution.py:122
  (201 shorter events, 48.3 us)
Async XLA Ops:
  8.7 15.6 %all-to-all-start.1 = ((s32[16,1,1]{2,1,0:T(1,128)}), s32[16,1,1]{2,1,0:T(1,128)S(1)}, u32[]{:S(2)}, u32[]{:S(2)}) async-start(s32[16,1,1]{2,1,0:T(1,128)} %copy.22), calls=%async_computation.1 | async-start | bytes 16384 | tf_op jit(solution)/shard_map/all_to_all | solution.py:99
  24.3 59.8 %all-to-all-start = ((bf16[16,4,256,128]{3,2,1,0:T(8,128)(2,1)}), bf16[16,4,256,128]{3,2,1,0:T(8,128)(2,1)}, u32[]{:S(2)}, u32[]{:S(2)}) async-start(bf16[16,4,256,128]{3,2,1,0:T(8,128)(2,1)} %copy.21), calls=%async_computation | async-start | bytes 8388608 | tf_op jit(solution)/shard_map/all_to_all | solution.py:98
  30.6 57.4 %copy-start.1 = (f32[4,512]{1,0:T(4,128)S(1)}, f32[4,512]{1,0:T(4,128)}, u32[]{:S(2)}) copy-start(f32[4,512]{1,0:T(4,128)} %param.10) | copy-start | bytes 24580
  30.6 113.3 %all-gather.2.cloned.1.call-start = ((), (), s32[]{:S(2)}) async-start(), calls=%async_computation.2 | async-start | bytes 2228224 | tf_op jit(solution)/shard_map/all_gather | solution.py:118
  84.2 63.9 %copy-start = (f32[3,256]{1,0:T(4,128)S(1)}, f32[3,256]{1,0:T(4,128)}, u32[]{:S(2)}) copy-start(f32[3,256]{1,0:T(4,128)} %param.11) | copy-start | bytes 9220
Sparse Core Ops, SparseCore 0:
  88.1 55.7 all-gather.1
where the time goes:
time: 538 us; the launch traced here: 537 us
  other arithmetic  324 us (60%)
  waiting for transfers between devices  81 us (15%)
  blocking collectives  62 us (12%)
  local copies, waits for them, and re-layouts  35.4 us (7%)
  starting transfers between devices  14.3 us (3%)
  between operations  14.1 us (3%)
    reduce_sum x16, other arithmetic, pressure_tiles(): press_re = jnp.sum(green_re * bracket_re - green_im * bracket_im, axis=2)  312 us
    all_to_all x1, waiting for transfers between devices, local(): lax.all_to_all(outgoing, 'obs', split_axis=0, concat_axis=0, tiled=True)  52.9 us
    psum x1, blocking collectives, local(): summed = lax.psum(pressure, 'grp')  33.3 us
    all_gather x1, blocking collectives, local(): lax.all_gather(face_geom, 'obs', axis=1, tiled=True)  28.8 us
    all_gather x1, waiting for transfers between devices, local(): lax.all_gather(spec_wide, 'obs', axis=1, tiled=True)  27.1 us
    dynamic_slice x32, local copies, waits for them, and re-layouts, accumulate(): result, _ = lax.scan(add_block, zero_sum, (spec_blocks, geom_blocks))  21.7 us
  transfers between devices with their start and end apart: 3, of which 3 were waited for; matrix products, arithmetic and copies ran while one was open for 1% of the time, Pallas kernels for 0%

commit v1 on v0

--- a/solution.py
+++ b/solution.py
@@ -115,7 +115,9 @@
     spec_wide = face_spec.astype(jnp.float32)
     pressure = accumulate(
         obs_pos,
-        lax.all_gather(spec_wide, "obs", axis=1, tiled=True),
+        jnp.concatenate(
+            lax.all_to_all(jnp.stack([spec_wide] * lax.axis_size("obs")), "obs", 0, 0), axis=1
+        ),
         lax.all_gather(face_geom, "obs", axis=1, tiled=True),
     )
     rows_out = 2 * NFREQ // lax.axis_size("grp")

time: 538 us -> 514 us (0.955)
  waiting for transfers between devices: 81 us -> 54 us
  blocking collectives: 62 us -> 76.4 us
  between operations: 14.1 us -> 0.76 us
  starting transfers between devices: 14.3 us -> 27.2 us
  local copies, waits for them, and re-layouts: 35.4 us -> 25.2 us
    all_gather x1 -> x0, waiting for transfers between devices: 27.1 us -> none  [local(): lax.all_gather(spec_wide, 'obs', axis=1, tiled=True)]
    all_gather x1, blocking collectives: 28.8 us -> 42.7 us  [local(): lax.all_gather(face_geom, 'obs', axis=1, tiled=True)]
    all_to_all x0 -> x1, starting transfers between devices: none -> 12.9 us  [local(): lax.all_to_all(jnp.stack([spec_wide] * lax.axis_size('obs')), 'obs', 0, 0)]
    dynamic_slice x32 -> x16, local copies, waits for them, and re-layouts: 21.7 us -> 14.7 us  [accumulate(): result, _ = lax.scan(add_block, zero_sum, (spec_blocks, geom_blocks))]
  transfers between devices with their start and end apart: 3 -> 3, of which waited for: 3 -> 2; matrix products, arithmetic and copies ran while one was open for 1% -> 1% of each run, Pallas kernels for 0% -> 0%
where the time goes in v1:
time: 514 us; the launch traced here: 513 us
  other arithmetic  324 us (63%)
  blocking collectives  76.4 us (15%)
  waiting for transfers between devices  54 us (11%)
  starting transfers between devices  27.2 us (5%)
  local copies, waits for them, and re-layouts  25.2 us (5%)
    reduce_sum x16, other arithmetic, pressure_tiles(): press_re = jnp.sum(green_re * bracket_re - green_im * bracket_im, axis=2)  312 us
    all_to_all x1, waiting for transfers between devices, local(): lax.all_to_all(outgoing, 'obs', split_axis=0, concat_axis=0, tiled=True)  53 us
    all_gather x1, blocking collectives, local(): lax.all_gather(face_geom, 'obs', axis=1, tiled=True)  42.7 us
    psum x1, blocking collectives, local(): summed = lax.psum(pressure, 'grp')  33.7 us
    dynamic_slice x16, local copies, waits for them, and re-layouts, accumulate(): result, _ = lax.scan(add_block, zero_sum, (spec_blocks, geom_blocks))  14.7 us
    all_to_all x1, starting transfers between devices, local(): lax.all_to_all(jnp.stack([spec_wide] * lax.axis_size('obs')), 'obs', 0, 0)  12.9 us
  transfers between devices with their start and end apart: 3, of which 2 were waited for; matrix products, arithmetic and copies ran while one was open for 1% of the time, Pallas kernels for 0%

profile of v1, /device:TPU:0, one launch (start us, length us, event | category | flops | bytes accessed | tf_op | source)
XLA Modules:
  0.0 513.0 jit_solution(12713163079595226304)
XLA Ops:
  2.2 8.0 %all-to-all-start.1 = ((s32[16,1,1]{2,1,0:T(1,128)}), s32[16,1,1]{2,1,0:T(1,128)S(1)}, u32[]{:S(2)}, u32[]{:S(2)}) async-start(s32[16,1,1]{2,1,0:T(1,128)} %copy.16), calls=%async_computation.1 | async-start | bytes 16384 | tf_op jit(solution)/shard_map/all_to_all | solution.py:99
  13.8 3.0 copy.15
  17.8 6.3 %all-to-all-start = ((bf16[16,4,256,128]{3,2,1,0:T(8,128)(2,1)}), bf16[16,4,256,128]{3,2,1,0:T(8,128)(2,1)}, u32[]{:S(2)}, u32[]{:S(2)}) async-start(bf16[16,4,256,128]{3,2,1,0:T(8,128)(2,1)} %copy.15), calls=%async_computation | async-start | bytes 8388608 | tf_op jit(solution)/shard_map/all_to_all | solution.py:98
  24.6 53.0 %all-to-all-done = bf16[16,4,256,128]{3,2,1,0:T(8,128)(2,1)} async-done(((bf16[16,4,256,128]{3,2,1,0:T(8,128)(2,1)}), bf16[16,4,256,128]{3,2,1,0:T(8,128)(2,1)}, u32[]{:S(2)}, u32[]{:S(2)}) %all-to-all-start) | async-done | bytes 4194336 | tf_op jit(solution)/shard_map/all_to_all | solution.py:98
  82.3 12.9 %all-to-all-start.2 = ((f32[16,64,512]{2,1,0:T(8,128)}), f32[16,64,512]{2,1,0:T(8,128)}, u32[]{:S(2)}, u32[]{:S(2)}) async-start(f32[16,64,512]{2,1,0:T(8,128)} %stack.2), calls=%async_computation.2 | async-start | bytes 4194304 | tf_op jit(solution)/shard_map/all_to_all | solution.py:119
  95.2 42.7 %all_gather.3 = f32[4,8192]{1,0:T(4,128)S(1)} all-gather(f32[4,512]{1,0:T(4,128)S(1)} %copy-done.1), channel_id=1, replica_groups=mesh['grp'=8,'obs'=16] {'obs'}, dimensions={1}, use_global_device_ids=true | all-gather | bytes 139264 | tf_op jit(solution)/shard_map/all_gather | solution.py:121
  137.9 340.9 %while.11 = (s32[]{:T(128)}, f32[16,256]{1,0:T(8,128)S(1)}, f32[16,4,512]{2,1,0:T(4,128)S(1)}, f32[3,256]{1,0:T(4,128)S(1)}, f32[16,64,512]{2,1,0:T(8,128)}, /*index=5*/s32[]{:T(128)}, s32[]{:T(128)}, s32[]{}) while((s32[]{:T(128)}, f32[16,256]{1,0:T(8,128)S(1)}, f32[16,4,512]{2,1,0:T(4,128)S(1)}, f32[3,256]{1,0:T(4,128)S(1)}, ...), condition=%wide.region_6.7_spmd.clone, body=%wide.region_2.6_spmd.clone.sunk | while | flops 31997980 | bytes 12283163 | solution.py:75
  139.6 19.5 %fusion.38 = (f32[8,256]{1,0:T(8,128)S(1)}, f32[8,256]{1,0:T(8,128)S(1)}) fusion(f32[8,512]{1,0:T(8,128)S(1)} %get-tuple-element.142, f32[256,512]{1,0:T(8,128)S(1)} %get-tuple-element.144, f32[8,512]{1,0:T(8,128)S(1)} %get-tuple-element.145, f32[8,512]{1,0:T(8,128)S(1)} %get-tuple-element.146, f32[8,512]{1,0:T(8,128)S(1)} %get-tuple-element.147, ...), kind=kLoop, calls=%fused_computation.8.clone.1 | loop fusion | flops 30404608 | bytes 3817504 | tf_op jit(solution)/shard_map/while/body/eval_jaxpr/reduce_sum | solution.py:55
  160.9 19.5 %fusion.38 = (f32[8,256]{1,0:T(8,128)S(1)}, f32[8,256]{1,0:T(8,128)S(1)}) fusion(f32[8,512]{1,0:T(8,128)S(1)} %get-tuple-element.142, f32[256,512]{1,0:T(8,128)S(1)} %get-tuple-element.144, f32[8,512]{1,0:T(8,128)S(1)} %get-tuple-element.145, f32[8,512]{1,0:T(8,128)S(1)} %get-tuple-element.146, f32[8,512]{1,0:T(8,128)S(1)} %get-tuple-element.147, ...), kind=kLoop, calls=%fused_computation.8.clone.1 | loop fusion | flops 30404608 | bytes 3817504 | tf_op jit(solution)/shard_map/while/body/eval_jaxpr/reduce_sum | solution.py:55
  182.2 19.5 %fusion.38 = (f32[8,256]{1,0:T(8,128)S(1)}, f32[8,256]{1,0:T(8,128)S(1)}) fusion(f32[8,512]{1,0:T(8,128)S(1)} %get-tuple-element.142, f32[256,512]{1,0:T(8,128)S(1)} %get-tuple-element.144, f32[8,512]{1,0:T(8,128)S(1)} %get-tuple-element.145, f32[8,512]{1,0:T(8,128)S(1)} %get-tuple-element.146, f32[8,512]{1,0:T(8,128)S(1)} %get-tuple-element.147, ...), kind=kLoop, calls=%fused_computation.8.clone.1 | loop fusion | flops 30404608 | bytes 3817504 | tf_op jit(solution)/shard_map/while/body/eval_jaxpr/reduce_sum | solution.py:55
  203.5 19.5 %fusion.38 = (f32[8,256]{1,0:T(8,128)S(1)}, f32[8,256]{1,0:T(8,128)S(1)}) fusion(f32[8,512]{1,0:T(8,128)S(1)} %get-tuple-element.142, f32[256,512]{1,0:T(8,128)S(1)} %get-tuple-element.144, f32[8,512]{1,0:T(8,128)S(1)} %get-tuple-element.145, f32[8,512]{1,0:T(8,128)S(1)} %get-tuple-element.146, f32[8,512]{1,0:T(8,128)S(1)} %get-tuple-element.147, ...), kind=kLoop, calls=%fused_computation.8.clone.1 | loop fusion | flops 30404608 | bytes 3817504 | tf_op jit(solution)/shard_map/while/body/eval_jaxpr/reduce_sum | solution.py:55
  224.8 19.5 %fusion.38 = (f32[8,256]{1,0:T(8,128)S(1)}, f32[8,256]{1,0:T(8,128)S(1)}) fusion(f32[8,512]{1,0:T(8,128)S(1)} %get-tuple-element.142, f32[256,512]{1,0:T(8,128)S(1)} %get-tuple-element.144, f32[8,512]{1,0:T(8,128)S(1)} %get-tuple-element.145, f32[8,512]{1,0:T(8,128)S(1)} %get-tuple-element.146, f32[8,512]{1,0:T(8,128)S(1)} %get-tuple-element.147, ...), kind=kLoop, calls=%fused_computation.8.clone.1 | loop fusion | flops 30404608 | bytes 3817504 | tf_op jit(solution)/shard_map/while/body/eval_jaxpr/reduce_sum | solution.py:55
  246.1 19.5 %fusion.38 = (f32[8,256]{1,0:T(8,128)S(1)}, f32[8,256]{1,0:T(8,128)S(1)}) fusion(f32[8,512]{1,0:T(8,128)S(1)} %get-tuple-element.142, f32[256,512]{1,0:T(8,128)S(1)} %get-tuple-element.144, f32[8,512]{1,0:T(8,128)S(1)} %get-tuple-element.145, f32[8,512]{1,0:T(8,128)S(1)} %get-tuple-element.146, f32[8,512]{1,0:T(8,128)S(1)} %get-tuple-element.147, ...), kind=kLoop, calls=%fused_computation.8.clone.1 | loop fusion | flops 30404608 | bytes 3817504 | tf_op jit(solution)/shard_map/while/body/eval_jaxpr/reduce_sum | solution.py:55
  267.4 19.5 %fusion.38 = (f32[8,256]{1,0:T(8,128)S(1)}, f32[8,256]{1,0:T(8,128)S(1)}) fusion(f32[8,512]{1,0:T(8,128)S(1)} %get-tuple-element.142, f32[256,512]{1,0:T(8,128)S(1)} %get-tuple-element.144, f32[8,512]{1,0:T(8,128)S(1)} %get-tuple-element.145, f32[8,512]{1,0:T(8,128)S(1)} %get-tuple-element.146, f32[8,512]{1,0:T(8,128)S(1)} %get-tuple-element.147, ...), kind=kLoop, calls=%fused_computation.8.clone.1 | loop fusion | flops 30404608 | bytes 3817504 | tf_op jit(solution)/shard_map/while/body/eval_jaxpr/reduce_sum | solution.py:55
  288.8 19.5 %fusion.38 = (f32[8,256]{1,0:T(8,128)S(1)}, f32[8,256]{1,0:T(8,128)S(1)}) fusion(f32[8,512]{1,0:T(8,128)S(1)} %get-tuple-element.142, f32[256,512]{1,0:T(8,128)S(1)} %get-tuple-element.144, f32[8,512]{1,0:T(8,128)S(1)} %get-tuple-element.145, f32[8,512]{1,0:T(8,128)S(1)} %get-tuple-element.146, f32[8,512]{1,0:T(8,128)S(1)} %get-tuple-element.147, ...), kind=kLoop, calls=%fused_computation.8.clone.1 | loop fusion | flops 30404608 | bytes 3817504 | tf_op jit(solution)/shard_map/while/body/eval_jaxpr/reduce_sum | solution.py:55
  310.1 19.5 %fusion.38 = (f32[8,256]{1,0:T(8,128)S(1)}, f32[8,256]{1,0:T(8,128)S(1)}) fusion(f32[8,512]{1,0:T(8,128)S(1)} %get-tuple-element.142, f32[256,512]{1,0:T(8,128)S(1)} %get-tuple-element.144, f32[8,512]{1,0:T(8,128)S(1)} %get-tuple-element.145, f32[8,512]{1,0:T(8,128)S(1)} %get-tuple-element.146, f32[8,512]{1,0:T(8,128)S(1)} %get-tuple-element.147, ...), kind=kLoop, calls=%fused_computation.8.clone.1 | loop fusion | flops 30404608 | bytes 3817504 | tf_op jit(solution)/shard_map/while/body/eval_jaxpr/reduce_sum | solution.py:55
  331.4 19.5 %fusion.38 = (f32[8,256]{1,0:T(8,128)S(1)}, f32[8,256]{1,0:T(8,128)S(1)}) fusion(f32[8,512]{1,0:T(8,128)S(1)} %get-tuple-element.142, f32[256,512]{1,0:T(8,128)S(1)} %get-tuple-element.144, f32[8,512]{1,0:T(8,128)S(1)} %get-tuple-element.145, f32[8,512]{1,0:T(8,128)S(1)} %get-tuple-element.146, f32[8,512]{1,0:T(8,128)S(1)} %get-tuple-element.147, ...), kind=kLoop, calls=%fused_computation.8.clone.1 | loop fusion | flops 30404608 | bytes 3817504 | tf_op jit(solution)/shard_map/while/body/eval_jaxpr/reduce_sum | solution.py:55
  352.7 19.5 %fusion.38 = (f32[8,256]{1,0:T(8,128)S(1)}, f32[8,256]{1,0:T(8,128)S(1)}) fusion(f32[8,512]{1,0:T(8,128)S(1)} %get-tuple-element.142, f32[256,512]{1,0:T(8,128)S(1)} %get-tuple-element.144, f32[8,512]{1,0:T(8,128)S(1)} %get-tuple-element.145, f32[8,512]{1,0:T(8,128)S(1)} %get-tuple-element.146, f32[8,512]{1,0:T(8,128)S(1)} %get-tuple-element.147, ...), kind=kLoop, calls=%fused_computation.8.clone.1 | loop fusion | flops 30404608 | bytes 3817504 | tf_op jit(solution)/shard_map/while/body/eval_jaxpr/reduce_sum | solution.py:55
  374.0 19.5 %fusion.38 = (f32[8,256]{1,0:T(8,128)S(1)}, f32[8,256]{1,0:T(8,128)S(1)}) fusion(f32[8,512]{1,0:T(8,128)S(1)} %get-tuple-element.142, f32[256,512]{1,0:T(8,128)S(1)} %get-tuple-element.144, f32[8,512]{1,0:T(8,128)S(1)} %get-tuple-element.145, f32[8,512]{1,0:T(8,128)S(1)} %get-tuple-element.146, f32[8,512]{1,0:T(8,128)S(1)} %get-tuple-element.147, ...), kind=kLoop, calls=%fused_computation.8.clone.1 | loop fusion | flops 30404608 | bytes 3817504 | tf_op jit(solution)/shard_map/while/body/eval_jaxpr/reduce_sum | solution.py:55
  395.3 19.5 %fusion.38 = (f32[8,256]{1,0:T(8,128)S(1)}, f32[8,256]{1,0:T(8,128)S(1)}) fusion(f32[8,512]{1,0:T(8,128)S(1)} %get-tuple-element.142, f32[256,512]{1,0:T(8,128)S(1)} %get-tuple-element.144, f32[8,512]{1,0:T(8,128)S(1)} %get-tuple-element.145, f32[8,512]{1,0:T(8,128)S(1)} %get-tuple-element.146, f32[8,512]{1,0:T(8,128)S(1)} %get-tuple-element.147, ...), kind=kLoop, calls=%fused_computation.8.clone.1 | loop fusion | flops 30404608 | bytes 3817504 | tf_op jit(solution)/shard_map/while/body/eval_jaxpr/reduce_sum | solution.py:55
  416.6 19.5 %fusion.38 = (f32[8,256]{1,0:T(8,128)S(1)}, f32[8,256]{1,0:T(8,128)S(1)}) fusion(f32[8,512]{1,0:T(8,128)S(1)} %get-tuple-element.142, f32[256,512]{1,0:T(8,128)S(1)} %get-tuple-element.144, f32[8,512]{1,0:T(8,128)S(1)} %get-tuple-element.145, f32[8,512]{1,0:T(8,128)S(1)} %get-tuple-element.146, f32[8,512]{1,0:T(8,128)S(1)} %get-tuple-element.147, ...), kind=kLoop, calls=%fused_computation.8.clone.1 | loop fusion | flops 30404608 | bytes 3817504 | tf_op jit(solution)/shard_map/while/body/eval_jaxpr/reduce_sum | solution.py:55
  437.9 19.5 %fusion.38 = (f32[8,256]{1,0:T(8,128)S(1)}, f32[8,256]{1,0:T(8,128)S(1)}) fusion(f32[8,512]{1,0:T(8,128)S(1)} %get-tuple-element.142, f32[256,512]{1,0:T(8,128)S(1)} %get-tuple-element.144, f32[8,512]{1,0:T(8,128)S(1)} %get-tuple-element.145, f32[8,512]{1,0:T(8,128)S(1)} %get-tuple-element.146, f32[8,512]{1,0:T(8,128)S(1)} %get-tuple-element.147, ...), kind=kLoop, calls=%fused_computation.8.clone.1 | loop fusion | flops 30404608 | bytes 3817504 | tf_op jit(solution)/shard_map/while/body/eval_jaxpr/reduce_sum | solution.py:55
  459.2 19.5 %fusion.38 = (f32[8,256]{1,0:T(8,128)S(1)}, f32[8,256]{1,0:T(8,128)S(1)}) fusion(f32[8,512]{1,0:T(8,128)S(1)} %get-tuple-element.142, f32[256,512]{1,0:T(8,128)S(1)} %get-tuple-element.144, f32[8,512]{1,0:T(8,128)S(1)} %get-tuple-element.145, f32[8,512]{1,0:T(8,128)S(1)} %get-tuple-element.146, f32[8,512]{1,0:T(8,128)S(1)} %get-tuple-element.147, ...), kind=kLoop, calls=%fused_computation.8.clone.1 | loop fusion | flops 30404608 | bytes 3817504 | tf_op jit(solution)/shard_map/while/body/eval_jaxpr/reduce_sum | solution.py:55
  478.8 33.7 %psum.7 = f32[16,256]{1,0:T(8,128)S(1)} all-reduce(f32[16,256]{1,0:T(8,128)S(1)} %get-tuple-element.32), channel_id=1, replica_groups=mesh['grp'=8,'obs'=16] {'grp'}, use_global_device_ids=true, to_apply=%region_7.8 | all-reduce | flops 4096 | bytes 32768 | tf_op jit(solution)/shard_map/psum | solution.py:124
  (184 shorter events, 39.2 us)
Async XLA Ops:
  2.2 15.6 %all-to-all-start.1 = ((s32[16,1,1]{2,1,0:T(1,128)}), s32[16,1,1]{2,1,0:T(1,128)S(1)}, u32[]{:S(2)}, u32[]{:S(2)}) async-start(s32[16,1,1]{2,1,0:T(1,128)} %copy.16), calls=%async_computation.1 | async-start | bytes 16384 | tf_op jit(solution)/shard_map/all_to_all | solution.py:99
  17.8 59.8 %all-to-all-start = ((bf16[16,4,256,128]{3,2,1,0:T(8,128)(2,1)}), bf16[16,4,256,128]{3,2,1,0:T(8,128)(2,1)}, u32[]{:S(2)}, u32[]{:S(2)}) async-start(bf16[16,4,256,128]{3,2,1,0:T(8,128)(2,1)} %copy.15), calls=%async_computation | async-start | bytes 8388608 | tf_op jit(solution)/shard_map/all_to_all | solution.py:98
  80.5 14.7 %copy-start.1 = (f32[4,512]{1,0:T(4,128)S(1)}, f32[4,512]{1,0:T(4,128)}, u32[]{:S(2)}) copy-start(f32[4,512]{1,0:T(4,128)} %param.10) | copy-start | bytes 24580
  80.5 57.4 %copy-start = (f32[3,256]{1,0:T(4,128)S(1)}, f32[3,256]{1,0:T(4,128)}, u32[]{:S(2)}) copy-start(f32[3,256]{1,0:T(4,128)} %param.11) | copy-start | bytes 9220
  82.3 55.6 %all-to-all-start.2 = ((f32[16,64,512]{2,1,0:T(8,128)}), f32[16,64,512]{2,1,0:T(8,128)}, u32[]{:S(2)}, u32[]{:S(2)}) async-start(f32[16,64,512]{2,1,0:T(8,128)} %stack.2), calls=%async_computation.2 | async-start | bytes 4194304 | tf_op jit(solution)/shard_map/all_to_all | solution.py:119
